TPU v7x, 32 devices: a whole 2x2x4 slice. The times are simulated.
32 devices in a mesh: cuts: 2 (over x), mode: 16 (over z, y, core).
Axes of the slice: x: 2, y: 2, z: 4, core: 2. Of those that a mesh axis runs over, the one named last changes fastest.
Arguments:
- stem_tensor: float32 [2, 2, 16, 512, 512], P(None, 'cuts', 'mode'), parts along dimension 1, may hold values from -6 to 6
- branch_tensors: float32 [4, 2, 512, 512], replicated, may hold values from -0.1875 to 0.1875
- branch_order: int32 [4], replicated, may hold values from 0 to 3, each once
Outputs:
- new_stem: float32 [2, 2, 16, 512, 512], P(None, 'cuts', 'mode'), parts along dimension 1
There are 2 independent parts, one for each index of `cuts`. A program takes and returns all parts, laid end to end along the dimension named above; an argument that names none is the same for every part. Nothing has to cross between parts.
Inputs may be any that keep to these rules, and one draw needn't show every extreme that they name: `branch_order`: a permutation of the 4 branch tensors.
All inputs are finite; a program needn't handle non-finite values.
Results may differ from a plain program's by a relative error of at most 0.00007.
Values sent between devices are 32-bit elements; how exact they have to be, the bound alone decides.
A program may use at most 64 MiB of HBM per device.

v0:
```python
import jax
import jax.numpy as jnp
from jax import lax
from jax.sharding import PartitionSpec as P


def complex_product(first, second, form):
    high = lax.Precision.HIGHEST
    real = jnp.einsum(form, first[0], second[0], precision=high) - jnp.einsum(
        form, first[1], second[1], precision=high
    )
    imag = jnp.einsum(form, first[0], second[1], precision=high) + jnp.einsum(
        form, first[1], second[0], precision=high
    )
    return jnp.stack([real, imag])


def on_device(stem_tensor, branch_tensors, branch_order):
    field = stem_tensor[:, :, 0]
    chosen = [branch_tensors[branch_order[index]] for index in range(4)]
    field = complex_product(field, chosen[0], "sce,cd->sde")
    field = complex_product(field, chosen[1], "sce,ed->scd")
    moved = lax.all_to_all(field[:, :, None], "mode", split_axis=3, concat_axis=2, tiled=True)
    merged = moved.reshape(field.shape)
    merged = complex_product(merged, chosen[2], "sce,cd->sde")
    return complex_product(merged, chosen[3], "sce,ed->scd")[:, :, None]


def solution(mesh):
    return jax.shard_map(
        on_device,
        mesh=mesh,
        in_specs=(P(None, "cuts", "mode", None, None), P(), P()),
        out_specs=P(None, "cuts", "mode", None, None),
        check_vma=False,
    )
```

profile of v0, /device:TPU:13, one launch (start us, length us, event | category | flops | bytes accessed | tf_op | source)
XLA Modules:
  0.0 113.0 jit_solution(4636353543271433322)
XLA Ops:
  0.0 1.5 %fusion.45 = (s32[1]{0:T(128)}, s32[1]{0:T(128)}, s32[1]{0:T(128)}, s32[1]{0:T(128)}) fusion(s32[4]{0:T(128)} %param.5), kind=kLoop, calls=%fused_computation.63 | loop fusion | bytes 32 | tf_op jit(solution)/shard_map/slice | solution.py:20
  4.7 0.0 copy-start
  4.7 3.5 %fusion.14 = f32[512,512]{1,0:T(8,128)S(1)} fusion(f32[2,1,1,512,512]{4,3,2,1,0:T(8,128)} %param.3, f32[4,2,512,512]{3,2,1,0:T(8,128)} %param.4, s32[]{:T(128)S(6)} %select_n.13), kind=kOutput, calls=%fused_computation.32 | convolution fusion | flops 1610612736 | bytes 3145732 | tf_op jit(solution)/shard_map/sce,cd->sde/dot_general | solution.py:9
  8.2 4.4 %fusion.12 = f32[512,512]{1,0:T(8,128)} fusion(f32[2,1,1,512,512]{4,3,2,1,0:T(8,128)} %param.3, f32[4,2,512,512]{3,2,1,0:T(8,128)} %param.4, s32[]{:T(128)S(6)} %select_n.13, s32[]{:T(128)S(6)} %add.36), kind=kOutput, calls=%fused_computation.30 | convolution fusion | flops 1610612736 | bytes 3145736 | tf_op jit(solution)/shard_map/sce,cd->sde/dot_general | solution.py:12
  12.6 3.4 %convolution_subtract_fusion.3 = f32[512,512]{1,0:T(8,128)S(1)} fusion(f32[512,512]{1,0:T(8,128)S(1)} %fusion.14, f32[2,1,1,512,512]{4,3,2,1,0:T(8,128)} %param.3, f32[4,2,512,512]{3,2,1,0:T(8,128)} %param.4, s32[]{:T(128)S(6)} %select_n.13, s32[]{:T(128)S(6)} %add.36), kind=kOutput, calls=%fused_computation.13 | convolution fusion | flops 1610874880 | bytes 4194312 | tf_op jit(solution)/shard_map/sce,cd->sde/dot_general | solution.py:9
  16.6 3.1 %fusion.26 = f32[512,512]{1,0:T(8,128)S(1)} fusion(f32[512,512]{1,0:T(8,128)S(1)} %convolution_subtract_fusion.3, f32[4,2,512,512]{3,2,1,0:T(8,128)} %param.4, s32[]{:T(128)S(6)} %select_n.14, s32[]{:T(128)S(6)} %add.36), kind=kOutput, calls=%fused_computation.44 | convolution fusion | flops 1610612736 | bytes 3145736 | tf_op jit(solution)/shard_map/sce,ed->scd/dot_general | solution.py:12
  19.7 3.1 %fusion.24 = f32[512,512]{1,0:T(8,128)S(1)} fusion(f32[512,512]{1,0:T(8,128)S(1)} %convolution_subtract_fusion.3, f32[4,2,512,512]{3,2,1,0:T(8,128)} %param.4, s32[]{:T(128)S(6)} %select_n.14), kind=kOutput, calls=%fused_computation.42 | convolution fusion | flops 1610612736 | bytes 3145732 | tf_op jit(solution)/shard_map/sce,ed->scd/dot_general | solution.py:9
  22.8 0.0 copy-done
  22.8 3.4 %convolution_add_fusion.3 = f32[512,512]{1,0:T(8,128)S(1)} fusion(f32[512,512]{1,0:T(8,128)} %fusion.12, f32[2,1,1,512,512]{4,3,2,1,0:T(8,128)S(1)} %copy-done, f32[4,2,512,512]{3,2,1,0:T(8,128)} %param.4, s32[]{:T(128)S(6)} %select_n.13), kind=kOutput, calls=%fused_computation.12 | convolution fusion | flops 1610874880 | bytes 4194308 | tf_op jit(solution)/shard_map/sce,cd->sde/dot_general | solution.py:12
  26.2 3.3 %fusion.3 = f32[1,1,512,512]{3,2,1,0:T(8,128)S(1)} fusion(f32[512,512]{1,0:T(8,128)S(1)} %fusion.24, f32[512,512]{1,0:T(8,128)S(1)} %convolution_add_fusion.3, f32[4,2,512,512]{3,2,1,0:T(8,128)} %param.4, s32[]{:T(128)S(6)} %select_n.14, s32[]{:T(128)S(6)} %add.36), kind=kOutput, calls=%fused_computation.11 | convolution fusion | flops 1610874880 | bytes 4194312 | tf_op jit(solution)/shard_map/sce,ed->scd/dot_general | solution.py:9
  29.5 3.1 %fusion.2 = f32[1,1,512,512]{3,2,1,0:T(8,128)S(1)} fusion(f32[512,512]{1,0:T(8,128)S(1)} %fusion.26, f32[512,512]{1,0:T(8,128)S(1)} %convolution_add_fusion.3, f32[4,2,512,512]{3,2,1,0:T(8,128)} %param.4, s32[]{:T(128)S(6)} %select_n.14), kind=kOutput, calls=%fused_computation.9 | convolution fusion | flops 1610874880 | bytes 4194308 | tf_op jit(solution)/shard_map/sce,ed->scd/dot_general | solution.py:12
  32.6 0.2 maximum_bitcast_fusion
  32.7 2.9 %copy.5 = f32[2,1,1,512,512]{4,0,2,1,3:T(2,128)} copy(f32[2,1,1,512,512]{4,3,0,2,1:T(8,128)S(1)} %maximum_bitcast_fusion) | data formatting | bytes 4194304 | tf_op jit(solution)/shard_map/broadcast_in_dim | solution.py:23
  35.7 6.5 %all-to-all-start = ((f32[2,1,1,512,512]{4,0,2,1,3:T(2,128)}), f32[2,1,1,512,512]{4,0,2,1,3:T(2,128)S(1)}, u32[]{:S(2)}, u32[]{:S(2)}) async-start(f32[2,1,1,512,512]{4,0,2,1,3:T(2,128)} %copy.5), calls=%async_computation | async-start | bytes 4194304 | tf_op jit(solution)/shard_map/all_to_all | solution.py:23
  46.1 43.5 %all-to-all-done = f32[2,1,1,512,512]{4,0,2,1,3:T(2,128)S(1)} async-done(((f32[2,1,1,512,512]{4,0,2,1,3:T(2,128)}), f32[2,1,1,512,512]{4,0,2,1,3:T(2,128)S(1)}, u32[]{:S(2)}, u32[]{:S(2)}) %all-to-all-start) | async-done | bytes 2097184 | tf_op jit(solution)/shard_map/all_to_all | solution.py:23
  89.6 0.0 slice-start
  89.6 1.6 %fusion.44 = (f32[1,1,1,512,512]{4,0,2,1,3:T(1,128)S(1)}, f32[1,1,1,512,512]{4,0,2,1,3:T(1,128)S(1)}) fusion(f32[2,1,1,512,512]{4,0,2,1,3:T(2,128)S(1)} %all-to-all-done), kind=kLoop, calls=%fused_computation.62 | loop fusion | bytes 4194304 | tf_op jit(solution)/shard_map/slice | solution.py:10
  91.2 3.1 %fusion.6 = f32[512,512]{1,0:T(8,128)S(1)} fusion(f32[1,1,1,512,512]{4,0,2,1,3:T(1,128)S(1)} %get-tuple-element.6, f32[4,2,512,512]{3,2,1,0:T(8,128)} %param.4, s32[]{:T(128)S(6)} %select_n.12, s32[]{:T(128)S(6)} %add.36), kind=kOutput, calls=%fused_computation.24 | convolution fusion | flops 1610612736 | bytes 3145736 | tf_op jit(solution)/shard_map/sce,cd->sde/dot_general | solution.py:12
  94.3 0.0 slice-start.1
  94.3 3.2 %fusion.8 = f32[512,512]{1,0:T(8,128)S(1)} fusion(f32[1,1,1,512,512]{4,0,2,1,3:T(1,128)S(1)} %get-tuple-element.6, f32[4,2,512,512]{3,2,1,0:T(8,128)} %param.4, s32[]{:T(128)S(6)} %select_n.12), kind=kOutput, calls=%fused_computation.26 | convolution fusion | flops 1610612736 | bytes 3145732 | tf_op jit(solution)/shard_map/sce,cd->sde/dot_general | solution.py:9
  97.6 3.1 %convolution_subtract_fusion.1 = f32[512,512]{1,0:T(8,128)S(1)} fusion(f32[512,512]{1,0:T(8,128)S(1)} %fusion.8, f32[1,1,1,512,512]{4,0,2,1,3:T(1,128)S(1)} %get-tuple-element.5, f32[4,2,512,512]{3,2,1,0:T(8,128)} %param.4, s32[]{:T(128)S(6)} %select_n.12, s32[]{:T(128)S(6)} %add.36), kind=kOutput, calls=%fused_computation.7 | convolution fusion | flops 1610874880 | bytes 4194312 | tf_op jit(solution)/shard_map/sce,cd->sde/dot_general | solution.py:9
  100.7 3.1 %fusion.27 = f32[512,512]{1,0:T(8,128)S(1)} fusion(f32[512,512]{1,0:T(8,128)S(1)} %convolution_subtract_fusion.1, f32[4,2,512,512]{3,2,1,0:T(8,128)} %param.4, s32[]{:T(128)S(6)} %select_n.15, s32[]{:T(128)S(6)} %add.36), kind=kOutput, calls=%fused_computation.45 | convolution fusion | flops 1610612736 | bytes 3145736 | tf_op jit(solution)/shard_map/sce,ed->scd/dot_general | solution.py:12
  103.8 0.0 slice-done
  103.8 0.0 slice-done.1
  103.8 1.8 %fusion.25 = f32[512,512]{1,0:T(8,128)S(1)} fusion(f32[512,512]{1,0:T(8,128)S(1)} %convolution_subtract_fusion.1, f32[4,2,512,512]{3,2,1,0:T(8,128)S(1)} %bitcast.79, s32[]{:T(128)S(6)} %select_n.15), kind=kOutput, calls=%fused_computation.43 | convolution fusion | flops 1610612736 | bytes 3145732 | tf_op jit(solution)/shard_map/sce,ed->scd/dot_general | solution.py:9
  105.6 2.2 %convolution_add_fusion.1 = f32[512,512]{1,0:T(8,128)S(1)} fusion(f32[512,512]{1,0:T(8,128)S(1)} %fusion.6, f32[1,1,1,512,512]{4,0,2,1,3:T(1,128)S(1)} %get-tuple-element.5, f32[4,2,512,512]{3,2,1,0:T(8,128)S(1)} %bitcast.79, s32[]{:T(128)S(6)} %select_n.12), kind=kOutput, calls=%fused_computation.6 | convolution fusion | flops 1610874880 | bytes 4194308 | tf_op jit(solution)/shard_map/sce,cd->sde/dot_general | solution.py:12
  107.8 1.8 %fusion.1 = f32[1,1,512,512]{3,2,1,0:T(8,128)S(1)} fusion(f32[512,512]{1,0:T(8,128)S(1)} %fusion.25, f32[512,512]{1,0:T(8,128)S(1)} %convolution_add_fusion.1, f32[4,2,512,512]{3,2,1,0:T(8,128)S(1)} %bitcast.79, s32[]{:T(128)S(6)} %select_n.15, s32[]{:T(128)S(6)} %add.36), kind=kOutput, calls=%fused_computation.5 | convolution fusion | flops 1610874880 | bytes 4194312 | tf_op jit(solution)/shard_map/sce,ed->scd/dot_general | solution.py:9
  109.7 1.8 %fusion = f32[1,1,512,512]{3,2,1,0:T(8,128)S(1)} fusion(f32[512,512]{1,0:T(8,128)S(1)} %fusion.27, f32[512,512]{1,0:T(8,128)S(1)} %convolution_add_fusion.1, f32[4,2,512,512]{3,2,1,0:T(8,128)S(1)} %bitcast.79, s32[]{:T(128)S(6)} %select_n.15), kind=kOutput, calls=%fused_computation.3 | convolution fusion | flops 1610874880 | bytes 4194308 | tf_op jit(solution)/shard_map/sce,ed->scd/dot_general | solution.py:12
  111.5 1.5 %maximum_bitcast_fusion.1 = f32[2,1,1,512,512]{4,3,2,1,0:T(8,128)} fusion(f32[1,1,512,512]{3,2,1,0:T(8,128)S(1)} %fusion, f32[1,1,512,512]{3,2,1,0:T(8,128)S(1)} %fusion.1), kind=kLoop, calls=%fused_computation.1 | loop fusion | flops 524288 | bytes 4194304 | tf_op jit(solution)/shard_map/broadcast_in_dim | solution.py:26
  (1 shorter events, 0.0 us)
Async XLA Ops:
  4.7 18.1 %copy-start = (f32[2,1,1,512,512]{4,3,2,1,0:T(8,128)S(1)}, f32[2,1,1,512,512]{4,3,2,1,0:T(8,128)}, u32[]{:S(2)}) copy-start(f32[2,1,1,512,512]{4,3,2,1,0:T(8,128)} %param.3) | copy-start | bytes 6291460
  35.7 53.9 %all-to-all-start = ((f32[2,1,1,512,512]{4,0,2,1,3:T(2,128)}), f32[2,1,1,512,512]{4,0,2,1,3:T(2,128)S(1)}, u32[]{:S(2)}, u32[]{:S(2)}) async-start(f32[2,1,1,512,512]{4,0,2,1,3:T(2,128)} %copy.5), calls=%async_computation | async-start | bytes 4194304 | tf_op jit(solution)/shard_map/all_to_all | solution.py:23
  89.6 14.2 %slice-start = ((s8[8388608]{0:T(1024)(128)(4,1)}), s8[4194304]{0:T(1024)(128)(4,1)S(1)}, s32[]{:S(2)}) async-start(s8[8388608]{0:T(1024)(128)(4,1)} %bitcast.78), calls=%async_computation.1 | async-start | bytes 8388608
  94.3 9.4 %slice-start.1 = ((s8[8388608]{0:T(1024)(128)(4,1)}), s8[4194304]{0:T(1024)(128)(4,1)S(1)}, s32[]{:S(2)}) async-start(s8[8388608]{0:T(1024)(128)(4,1)} %bitcast.78), calls=%async_computation.2 | async-start | bytes 8388608
where the time goes:
time: 114 us; the launch traced here: 113 us
  matrix products  47.3 us (41%)
  waiting for transfers between devices  43.5 us (38%)
  between operations  7.96 us (7%)
  starting transfers between devices  6.52 us (6%)
  local copies, waits for them, and re-layouts  6.03 us (5%)
  other arithmetic  1.66 us (1%)
    all_to_all x1, waiting for transfers between devices, on_device(): lax.all_to_all(field[:, :, None], 'mode', split_axis=3, concat_axis=2, ti...  43.5 us
    dot_general x4, matrix products, complex_product(): jnp.einsum(form, first[0], second[1], precision=high)  13.6 us
    dot_general x4, matrix products, complex_product(): jnp.einsum(form, first[0], second[0], precision=high)  11.7 us
    dot_general x4, matrix products, complex_product(): jnp.einsum(form, first[1], second[1], precision=high)  11.6 us
    dot_general x4, matrix products, complex_product(): jnp.einsum(form, first[1], second[0], precision=high)  10.5 us
    all_to_all x1, starting transfers between devices, on_device(): lax.all_to_all(field[:, :, None], 'mode', split_axis=3, concat_axis=2, ti...  6.52 us
    broadcast_in_dim x1, local copies, waits for them, and re-layouts, on_device(): field[:, :, None]  2.94 us
  transfers between devices with their start and end apart: 1, of which 1 were waited for; matrix products, arithmetic and copies ran while one was open for 0% of the time, Pallas kernels for 0%

commit v1 on v0

--- a/solution.py
+++ b/solution.py
@@ -20,7 +20,11 @@
     chosen = [branch_tensors[branch_order[index]] for index in range(4)]
     field = complex_product(field, chosen[0], "sce,cd->sde")
     field = complex_product(field, chosen[1], "sce,ed->scd")
-    moved = lax.all_to_all(field[:, :, None], "mode", split_axis=3, concat_axis=2, tiled=True)
+    own = field[:, :, None]
+    n_dev = lax.axis_size("mode")
+    blocks = jnp.stack(jnp.split(own, n_dev, axis=3), axis=0)
+    blocks = lax.all_to_all(blocks, "mode", split_axis=0, concat_axis=0)
+    moved = jnp.concatenate(blocks, axis=2)
     merged = moved.reshape(field.shape)
     merged = complex_product(merged, chosen[2], "sce,cd->sde")
     return complex_product(merged, chosen[3], "sce,ed->scd")[:, :, None]

time: 114 us -> 119 us (1.044)
  local copies, waits for them, and re-layouts: 6.03 us -> 12.4 us
    unnamed x6 -> x23, local copies, waits for them, and re-layouts: 0.02 us -> 9.98 us
    broadcast_in_dim x1 -> x0, local copies, waits for them, and re-layouts: 2.94 us -> none  [on_device(): field[:, :, None]]
    slice x1, local copies, waits for them, and re-layouts: 1.62 us -> 0.26 us  [complex_product(): first[1]]
where the time goes in v1:
time: 119 us; the launch traced here: 118 us
  matrix products  46.4 us (39%)
  waiting for transfers between devices  43.6 us (37%)
  local copies, waits for them, and re-layouts  12.4 us (10%)
  between operations  7.8 us (7%)
  starting transfers between devices  6.52 us (5%)
  other arithmetic  1.66 us (1%)
    all_to_all x1, waiting for transfers between devices, on_device(): blocks = lax.all_to_all(blocks, 'mode', split_axis=0, concat_axis=0)  43.6 us
    dot_general x4, matrix products, complex_product(): jnp.einsum(form, first[0], second[1], precision=high)  13.4 us
    dot_general x4, matrix products, complex_product(): jnp.einsum(form, first[0], second[0], precision=high)  11.6 us
    dot_general x4, matrix products, complex_product(): jnp.einsum(form, first[1], second[1], precision=high)  11.5 us
    unnamed x23, local copies, waits for them, and re-layouts  9.98 us
    dot_general x4, matrix products, complex_product(): jnp.einsum(form, first[1], second[0], precision=high)  9.86 us
    all_to_all x1, starting transfers between devices, on_device(): blocks = lax.all_to_all(blocks, 'mode', split_axis=0, concat_axis=0)  6.52 us
  transfers between devices with their start and end apart: 1, of which 1 were waited for; matrix products, arithmetic and copies ran while one was open for 0% of the time, Pallas kernels for 0%

profile of v1, /device:TPU:13, one launch (start us, length us, event | category | flops | bytes accessed | tf_op | source)
XLA Modules:
  0.0 118.4 jit_solution(4246238176071900797)
XLA Ops:
  0.0 1.5 %fusion.53 = (s32[1]{0:T(128)}, s32[1]{0:T(128)}, s32[1]{0:T(128)}, s32[1]{0:T(128)}) fusion(s32[4]{0:T(128)} %param.5), kind=kLoop, calls=%fused_computation.87 | loop fusion | bytes 32 | tf_op jit(solution)/shard_map/slice | solution.py:20
  4.7 3.4 %fusion.8 = f32[512,512]{1,0:T(8,128)S(1)} fusion(f32[2,1,1,512,512]{4,3,2,1,0:T(8,128)} %param.3, f32[4,2,512,512]{3,2,1,0:T(8,128)} %param.4, s32[]{:T(128)S(6)} %select_n.13), kind=kOutput, calls=%fused_computation.26 | convolution fusion | flops 1610612736 | bytes 3145732 | tf_op jit(solution)/shard_map/sce,cd->sde/dot_general | solution.py:9
  8.1 4.1 %fusion.6 = f32[512,512]{1,0:T(8,128)} fusion(f32[2,1,1,512,512]{4,3,2,1,0:T(8,128)S(1)} %copy-done, f32[4,2,512,512]{3,2,1,0:T(8,128)} %param.4, s32[]{:T(128)S(6)} %select_n.13, s32[]{:T(128)S(6)} %add.36), kind=kOutput, calls=%fused_computation.24 | convolution fusion | flops 1610612736 | bytes 3145736 | tf_op jit(solution)/shard_map/sce,cd->sde/dot_general | solution.py:12
  12.2 3.1 %convolution_subtract_fusion.3 = f32[512,512]{1,0:T(8,128)S(1)} fusion(f32[512,512]{1,0:T(8,128)S(1)} %fusion.8, f32[2,1,1,512,512]{4,3,2,1,0:T(8,128)S(1)} %copy-done, f32[4,2,512,512]{3,2,1,0:T(8,128)} %param.4, s32[]{:T(128)S(6)} %select_n.13, s32[]{:T(128)S(6)} %add.36), kind=kOutput, calls=%fused_computation.13 | convolution fusion | flops 1610874880 | bytes 4194312 | tf_op jit(solution)/shard_map/sce,cd->sde/dot_general | solution.py:9
  15.9 3.1 %fusion.17 = f32[512,512]{1,0:T(8,128)S(1)} fusion(f32[512,512]{1,0:T(8,128)S(1)} %convolution_subtract_fusion.3, f32[4,2,512,512]{3,2,1,0:T(8,128)} %param.4, s32[]{:T(128)S(6)} %select_n.14, s32[]{:T(128)S(6)} %add.36), kind=kOutput, calls=%fused_computation.35 | convolution fusion | flops 1610612736 | bytes 3145736 | tf_op jit(solution)/shard_map/sce,ed->scd/dot_general | solution.py:12
  19.0 3.2 %fusion.15 = f32[512,512]{1,0:T(8,128)S(1)} fusion(f32[512,512]{1,0:T(8,128)S(1)} %convolution_subtract_fusion.3, f32[4,2,512,512]{3,2,1,0:T(8,128)} %param.4, s32[]{:T(128)S(6)} %select_n.14), kind=kOutput, calls=%fused_computation.33 | convolution fusion | flops 1610612736 | bytes 3145732 | tf_op jit(solution)/shard_map/sce,ed->scd/dot_general | solution.py:9
  22.1 3.1 %convolution_add_fusion.3 = f32[512,512]{1,0:T(8,128)S(1)} fusion(f32[512,512]{1,0:T(8,128)S(1)} %copy-done.1, f32[2,1,1,512,512]{4,3,2,1,0:T(8,128)S(1)} %copy-done, f32[4,2,512,512]{3,2,1,0:T(8,128)} %param.4, s32[]{:T(128)S(6)} %select_n.13), kind=kOutput, calls=%fused_computation.12 | convolution fusion | flops 1610874880 | bytes 4194308 | tf_op jit(solution)/shard_map/sce,cd->sde/dot_general | solution.py:12
  25.2 3.3 %fusion.3 = f32[1,1,512,512]{3,2,1,0:T(8,128)S(1)} fusion(f32[512,512]{1,0:T(8,128)S(1)} %fusion.15, f32[512,512]{1,0:T(8,128)S(1)} %convolution_add_fusion.3, f32[4,2,512,512]{3,2,1,0:T(8,128)} %param.4, s32[]{:T(128)S(6)} %select_n.14, s32[]{:T(128)S(6)} %add.36), kind=kOutput, calls=%fused_computation.11 | convolution fusion | flops 1610874880 | bytes 4194312 | tf_op jit(solution)/shard_map/sce,ed->scd/dot_general | solution.py:9
  28.5 3.1 %fusion.2 = f32[1,1,512,512]{3,2,1,0:T(8,128)S(1)} fusion(f32[512,512]{1,0:T(8,128)S(1)} %fusion.17, f32[512,512]{1,0:T(8,128)S(1)} %convolution_add_fusion.3, f32[4,2,512,512]{3,2,1,0:T(8,128)} %param.4, s32[]{:T(128)S(6)} %select_n.14), kind=kOutput, calls=%fused_computation.9 | convolution fusion | flops 1610874880 | bytes 4194308 | tf_op jit(solution)/shard_map/sce,ed->scd/dot_general | solution.py:12
  31.8 0.7 fusion.35
  32.4 0.7 fusion.34
  33.1 0.7 fusion.33
  33.8 0.7 fusion.32
  34.4 0.7 fusion.31
  35.1 0.7 fusion.30
  35.7 0.7 fusion.29
  36.4 0.7 fusion.28
  37.1 0.7 fusion.27
  37.7 0.7 fusion.26
  38.4 0.7 fusion.25
  39.1 0.7 fusion.24
  42.4 6.5 %all-to-all-start = ((f32[16,2,1,1,32,512]{5,4,1,3,2,0:T(8,128)}), f32[16,2,1,1,32,512]{5,4,1,3,2,0:T(8,128)S(1)}, u32[]{:S(2)}, u32[]{:S(2)}) async-start(f32[16,2,1,1,32,512]{5,4,1,3,2,0:T(8,128)} %fusion.20), calls=%async_computation | async-start | bytes 4194304 | tf_op jit(solution)/shard_map/all_to_all | solution.py:26
  52.7 43.6 %all-to-all-done = f32[16,2,1,1,32,512]{5,4,1,3,2,0:T(8,128)S(1)} async-done(((f32[16,2,1,1,32,512]{5,4,1,3,2,0:T(8,128)}), f32[16,2,1,1,32,512]{5,4,1,3,2,0:T(8,128)S(1)}, u32[]{:S(2)}, u32[]{:S(2)}) %all-to-all-start) | async-done | bytes 2097184 | tf_op jit(solution)/shard_map/all_to_all | solution.py:26
  96.6 3.2 %fusion.18 = f32[512,512]{1,0:T(8,128)S(1)} fusion(f32[512,512]{1,0:T(8,128)S(1)} %bitcast.143, f32[4,2,512,512]{3,2,1,0:T(8,128)} %param.4, s32[]{:T(128)S(6)} %select_n.12, s32[]{:T(128)S(6)} %add.36), kind=kOutput, calls=%fused_computation.36 | convolution fusion | flops 1610612736 | bytes 3145736 | tf_op jit(solution)/shard_map/sce,cd->sde/dot_general | solution.py:12
  99.9 3.2 %fusion.14 = f32[512,512]{1,0:T(8,128)S(1)} fusion(f32[512,512]{1,0:T(8,128)S(1)} %bitcast.144, f32[4,2,512,512]{3,2,1,0:T(8,128)} %param.4, s32[]{:T(128)S(6)} %select_n.12), kind=kOutput, calls=%fused_computation.32 | convolution fusion | flops 1610612736 | bytes 3145732 | tf_op jit(solution)/shard_map/sce,cd->sde/dot_general | solution.py:9
  103.1 3.1 %convolution_subtract_fusion.1 = f32[512,512]{1,0:T(8,128)S(1)} fusion(f32[512,512]{1,0:T(8,128)S(1)} %fusion.14, f32[512,512]{1,0:T(8,128)S(1)} %bitcast.141, f32[4,2,512,512]{3,2,1,0:T(8,128)} %param.4, s32[]{:T(128)S(6)} %select_n.12, s32[]{:T(128)S(6)} %add.36), kind=kOutput, calls=%fused_computation.7 | convolution fusion | flops 1610874880 | bytes 4194312 | tf_op jit(solution)/shard_map/sce,cd->sde/dot_general | solution.py:9
  106.2 3.1 %fusion.19 = f32[512,512]{1,0:T(8,128)S(1)} fusion(f32[512,512]{1,0:T(8,128)S(1)} %convolution_subtract_fusion.1, f32[4,2,512,512]{3,2,1,0:T(8,128)} %param.4, s32[]{:T(128)S(6)} %select_n.15, s32[]{:T(128)S(6)} %add.36), kind=kOutput, calls=%fused_computation.37 | convolution fusion | flops 1610612736 | bytes 3145736 | tf_op jit(solution)/shard_map/sce,ed->scd/dot_general | solution.py:12
  109.3 1.8 %fusion.16 = f32[512,512]{1,0:T(8,128)S(1)} fusion(f32[512,512]{1,0:T(8,128)S(1)} %convolution_subtract_fusion.1, f32[4,2,512,512]{3,2,1,0:T(8,128)S(1)} %bitcast.140, s32[]{:T(128)S(6)} %select_n.15), kind=kOutput, calls=%fused_computation.34 | convolution fusion | flops 1610612736 | bytes 3145732 | tf_op jit(solution)/shard_map/sce,ed->scd/dot_general | solution.py:9
  111.1 1.9 %convolution_add_fusion.1 = f32[512,512]{1,0:T(8,128)S(1)} fusion(f32[512,512]{1,0:T(8,128)S(1)} %fusion.18, f32[512,512]{1,0:T(8,128)S(1)} %bitcast.142, f32[4,2,512,512]{3,2,1,0:T(8,128)S(1)} %bitcast.140, s32[]{:T(128)S(6)} %select_n.12), kind=kOutput, calls=%fused_computation.6 | convolution fusion | flops 1610874880 | bytes 4194308 | tf_op jit(solution)/shard_map/sce,cd->sde/dot_general | solution.py:12
  113.0 2.1 %fusion.1 = f32[1,1,512,512]{3,2,1,0:T(8,128)S(1)} fusion(f32[512,512]{1,0:T(8,128)S(1)} %fusion.16, f32[512,512]{1,0:T(8,128)S(1)} %convolution_add_fusion.1, f32[4,2,512,512]{3,2,1,0:T(8,128)S(1)} %bitcast.140, s32[]{:T(128)S(6)} %select_n.15, s32[]{:T(128)S(6)} %add.36), kind=kOutput, calls=%fused_computation.5 | convolution fusion | flops 1610874880 | bytes 4194312 | tf_op jit(solution)/shard_map/sce,ed->scd/dot_general | solution.py:9
  115.1 1.8 %fusion = f32[1,1,512,512]{3,2,1,0:T(8,128)S(1)} fusion(f32[512,512]{1,0:T(8,128)S(1)} %fusion.19, f32[512,512]{1,0:T(8,128)S(1)} %convolution_add_fusion.1, f32[4,2,512,512]{3,2,1,0:T(8,128)S(1)} %bitcast.140, s32[]{:T(128)S(6)} %select_n.15), kind=kOutput, calls=%fused_computation.3 | convolution fusion | flops 1610874880 | bytes 4194308 | tf_op jit(solution)/shard_map/sce,ed->scd/dot_general | solution.py:12
  117.0 1.5 %maximum_bitcast_fusion.1 = f32[2,1,1,512,512]{4,3,2,1,0:T(8,128)} fusion(f32[1,1,512,512]{3,2,1,0:T(8,128)S(1)} %fusion, f32[1,1,512,512]{3,2,1,0:T(8,128)S(1)} %fusion.1), kind=kLoop, calls=%fused_computation.1 | loop fusion | flops 524288 | bytes 4194304 | tf_op jit(solution)/shard_map/broadcast_in_dim | solution.py:30
  (15 shorter events, 3.1 us)
Async XLA Ops:
  0.0 8.1 %copy-start = (f32[2,1,1,512,512]{4,3,2,1,0:T(8,128)S(1)}, f32[2,1,1,512,512]{4,3,2,1,0:T(8,128)}, u32[]{:S(2)}) copy-start(f32[2,1,1,512,512]{4,3,2,1,0:T(8,128)} %param.3) | copy-start | bytes 6291460
  18.9 3.2 %copy-start.1 = (f32[512,512]{1,0:T(8,128)S(1)}, f32[512,512]{1,0:T(8,128)}, u32[]{:S(2)}) copy-start(f32[512,512]{1,0:T(8,128)} %fusion.6) | copy-start | bytes 3145732
  42.4 53.9 %all-to-all-start = ((f32[16,2,1,1,32,512]{5,4,1,3,2,0:T(8,128)}), f32[16,2,1,1,32,512]{5,4,1,3,2,0:T(8,128)S(1)}, u32[]{:S(2)}, u32[]{:S(2)}) async-start(f32[16,2,1,1,32,512]{5,4,1,3,2,0:T(8,128)} %fusion.20), calls=%async_computation | async-start | bytes 4194304 | tf_op jit(solution)/shard_map/all_to_all | solution.py:26
  96.3 12.9 %slice-start = ((s8[8388608]{0:T(1024)(128)(4,1)}), s8[4194304]{0:T(1024)(128)(4,1)S(1)}, s32[]{:S(2)}) async-start(s8[8388608]{0:T(1024)(128)(4,1)} %bitcast.139), calls=%async_computation.1 | async-start | bytes 8388608
  99.8 9.4 %slice-start.1 = ((s8[8388608]{0:T(1024)(128)(4,1)}), s8[4194304]{0:T(1024)(128)(4,1)S(1)}, s32[]{:S(2)}) async-start(s8[8388608]{0:T(1024)(128)(4,1)} %bitcast.139), calls=%async_computation.2 | async-start | bytes 8388608
